TPU v7x, 512 devices: a whole 4x8x8 slice. The times are simulated.
512 devices in a mesh: river: 16 (over y_hi, x, core), hours: 32 (over y_lo, z).
Axes of the slice: x: 4, y: 8 (y_hi: 2, y_lo: 4; y = y_hi * 4 + y_lo), z: 8, core: 2. Of those that a mesh axis runs over, the one named last changes fastest.
Arguments:
- release: float32 [160, 512, 512], P('river', 'hours'), may hold values from 0 to 1
- storage_dual: float32 [160, 512, 512], P('river', 'hours'), may hold values from -3 to 3
- demand_dual: float32 [512, 512], P('hours'), may hold values from -1 to 0
- cost: float32 [160, 512, 512], P('river', 'hours'), may hold values from -1.8 to 1.8
- inflow: float32 [160, 512, 512], P('river', 'hours'), may hold values from 0 to 1.2
- demand: float32 [512, 512], P('hours'), may hold values from 4.427189 to 8.221922
- storage_start: float32 [160], P('river'), may hold values from -0.5 to 0.5
- storage_low: float32 [160], P('river'), may hold values from -2 to -0.5
- storage_high: float32 [160], P('river'), may hold values from 0.5 to 2
- release_cap: float32 [160], P('river'), may hold values from 0.5 to 1.5
- efficiency: float32 [160], P('river'), may hold values from 0.5 to 1.5
- downstream: int32 [160], P('river'), may hold values from -1 to 159, as said below
- travel_delay: int32 [160], P('river'), may hold values from 1 to 6
Outputs:
- release_new: float32 [160, 512, 512], P('river', 'hours')
- storage_dual_new: float32 [160, 512, 512], P('river', 'hours')
- demand_dual_new: float32 [512, 512], P('hours')
- storage_excess: float32 [160, 512, 512], P('river', 'hours')
Inputs may be any that keep to these rules, and one draw needn't show every extreme that they name: Each reservoir's downstream index is -1 or lies 1 to 10 positions after its own index.
All inputs are finite; a program needn't handle non-finite values.
Results may differ from a plain program's by a relative error of at most 0.00013.
Values sent between devices are 32-bit elements; how exact they have to be, the bound alone decides.
A program may use at most 64 MiB of HBM per device.

v0:
```python
import math
import jax
import jax.numpy as jnp
from jax import lax
from jax.sharding import PartitionSpec as P

DMAX = 6
primal_step = 1.0
dual_step = 0.1


def passed_along(block, axis, distance):
    devices = range(lax.axis_size(axis))
    route = [(i - distance, i) for i in devices if i - distance in devices]
    return lax.ppermute(block, axis, route)


def prefix(part, axis, combine, identity, reverse):
    count = lax.axis_size(axis)
    place = lax.axis_index(axis)
    ahead = count - 1 - place if reverse else place
    gathered = lax.all_gather(part, axis)
    state = jnp.zeros_like(part) + jnp.asarray(identity, part.dtype)

    def one(turn, state):
        source = count - 1 - turn if reverse else turn
        return combine(state, lax.dynamic_index_in_dim(gathered, source, 0, False))

    return lax.fori_loop(0, ahead, one, state)


def add_pair(earlier_part, later_part):
    return earlier_part + later_part


def hold_back(field, travel_delay, earlier_rim):
    length = field.shape[1]
    extended = jnp.concatenate([earlier_rim, field], 1)
    result = jnp.zeros_like(field)
    for lag_hours in range(1, DMAX + 1):
        window = extended[:, DMAX - lag_hours : DMAX - lag_hours + length]
        result = result + jnp.where((travel_delay == lag_hours)[:, None, None], window, 0.0)
    return result


def bring_forward(field, travel_delay, later_rim):
    length = field.shape[1]
    extended = jnp.concatenate([field, later_rim], 1)
    result = jnp.zeros_like(field)
    for lag_hours in range(1, DMAX + 1):
        window = extended[:, lag_hours : lag_hours + length]
        result = result + jnp.where((travel_delay == lag_hours)[:, None, None], window, 0.0)
    return result


def route_down(matrix, field):
    return jnp.einsum("ij,jtw->itw", matrix, field, precision=lax.Precision.HIGHEST)


def route_up(matrix, field):
    return jnp.einsum("ij,itw->jtw", matrix, field, precision=lax.Precision.HIGHEST)


def iterate(fields, statics, scales, prefix_sum, suffix_sum, from_earlier, from_later):
    release, storage_dual, demand_dual, cost, inflow, demand = fields
    (
        storage_start,
        storage_low,
        storage_high,
        release_cap,
        efficiency,
        travel_delay,
        to_own,
        to_next,
    ) = statics
    scale_time, scale_sum = scales
    suffix = suffix_sum(storage_dual)
    beyond = passed_along(suffix, "river", -1)
    at_sink = route_up(to_own, suffix) + route_up(to_next, beyond)
    later_duals = bring_forward(at_sink, travel_delay, from_later(at_sink[:, :DMAX]))
    gradient = (
        cost
        + scale_time * (later_duals - suffix)
        + scale_sum * efficiency[:, None, None] * demand_dual[None]
    )
    release_new = jnp.clip(release - primal_step * gradient, 0.0, release_cap[:, None, None])
    extrapolated = 2.0 * release_new - release
    length = extrapolated.shape[1]
    delayed = hold_back(extrapolated, travel_delay, from_earlier(extrapolated[:, length - DMAX :]))
    incoming = passed_along(route_down(to_next, delayed), "river", 1)
    routed = route_down(to_own, delayed) + incoming
    storage = storage_start[:, None, None] + scale_time * prefix_sum(inflow + routed - extrapolated)
    lower_bound = storage_low[:, None, None]
    upper_bound = storage_high[:, None, None]
    storage_dual_new = (
        storage_dual
        + dual_step * storage
        - dual_step * jnp.clip(storage_dual / dual_step + storage, lower_bound, upper_bound)
    )
    storage_excess = storage - jnp.clip(storage, lower_bound, upper_bound)
    partial_power = jnp.sum(scale_sum * efficiency[:, None, None] * extrapolated, 0)
    supplied = lax.psum(partial_power, "river")
    demand_dual_new = jnp.minimum(demand_dual + dual_step * (supplied - demand), 0.0)
    return (release_new, storage_dual_new, demand_dual_new, storage_excess)


def suffix_local(field):
    return jnp.flip(jnp.cumsum(jnp.flip(field, 1), 1), 1)


def shards(
    release,
    storage_dual,
    demand_dual,
    cost,
    inflow,
    demand,
    storage_start,
    storage_low,
    storage_high,
    release_cap,
    efficiency,
    downstream,
    travel_delay,
):
    res_dev = release.shape[0]
    scale_time = 1.0 / (release.shape[1] * lax.axis_size("hours"))
    scale_sum = 1.0 / math.sqrt(res_dev * lax.axis_size("river"))
    base_index = lax.axis_index("river") * res_dev
    target = downstream - base_index
    indices = jnp.arange(res_dev, dtype=jnp.int32)
    to_own = (target[None, :] == indices[:, None]).astype(jnp.float32)
    to_next = (target[None, :] == indices[:, None] + res_dev).astype(jnp.float32)
    statics = (
        storage_start,
        storage_low,
        storage_high,
        release_cap,
        efficiency,
        travel_delay,
        to_own,
        to_next,
    )
    scales = (scale_time, scale_sum)

    def prefix_blocks(field):
        local_sum = jnp.cumsum(field, 1)
        totals = local_sum[:, -1]
        offset = prefix(totals, "hours", add_pair, jnp.zeros_like(totals), False)
        return local_sum + offset[:, None]

    def suffix_blocks(field):
        local_sum = suffix_local(field)
        totals = local_sum[:, 0]
        offset = prefix(totals, "hours", add_pair, jnp.zeros_like(totals), True)
        return local_sum + offset[:, None]

    def earlier_block(part):
        return passed_along(part, "hours", 1)

    def later_block(part):
        return passed_along(part, "hours", -1)

    fields = (release, storage_dual, demand_dual, cost, inflow, demand)
    return iterate(
        fields, statics, scales, prefix_blocks, suffix_blocks, earlier_block, later_block
    )


def solution(mesh):
    return jax.shard_map(
        shards,
        mesh=mesh,
        in_specs=(
            P("river", "hours", None),
            P("river", "hours", None),
            P("hours", None),
            P("river", "hours", None),
            P("river", "hours", None),
            P("hours", None),
            P("river"),
            P("river"),
            P("river"),
            P("river"),
            P("river"),
            P("river"),
            P("river"),
        ),
        out_specs=(
            P("river", "hours", None),
            P("river", "hours", None),
            P("hours", None),
            P("river", "hours", None),
        ),
        check_vma=False,
    )
```

profile of v0, /device:TPU:32, one launch (start us, length us, event | category | flops | bytes accessed | tf_op | source)
XLA Modules:
  0.0 301.1 jit_solution(5361114669511193955)
XLA Ops:
  0.6 1.8 rev.7
  2.5 0.4 fusion.45
  2.9 86.1 %all-gather = f32[320,1,512]{2,1,0:T(1,128)S(1)} all-gather(f32[10,1,512]{2,1,0:T(1,128)S(1)} %copy.42), channel_id=2, replica_groups=mesh['river'=16,'hours'=32] {'hours'}, dimensions={0}, use_global_device_ids=true | all-gather | bytes 675840 | tf_op jit(solution)/shard_map/all_gather | solution.py:22
  89.0 1.6 reduce
  90.7 1.2 while.22
  91.9 1.9 collective-permute-start
  93.8 0.6 copy-done.7
  94.5 0.6 copy-done.8
  95.2 0.4 fusion.49
  95.6 4.9 %collective-permute-done = f32[10,16,512]{2,0,1:T(8,128)S(1)} collective-permute-done((f32[10,16,512]{2,0,1:T(8,128)S(1)}, f32[10,16,512]{2,0,1:T(8,128)S(1)}, u32[]{:S(2)}, u32[]{:S(2)}) %collective-permute-start) | collective-permute-done | bytes 327712 | tf_op jit(solution)/shard_map/ppermute | solution.py:15
  100.5 0.5 convolution_add_fusion.1
  101.1 1.4 collective-permute-start.1
  102.5 7.7 %collective-permute-done.1 = f32[10,6,512]{2,0,1:T(8,128)S(1)} collective-permute-done((f32[10,6,512]{2,0,1:T(8,128)S(1)}, f32[10,6,512]{2,0,1:T(8,128)S(1)}, u32[]{:S(2)}, u32[]{:S(2)}) %collective-permute-start.1) | collective-permute-done | bytes 122912 | tf_op jit(solution)/shard_map/ppermute | solution.py:15
  110.2 0.6 copy-done.6
  110.9 0.8 multiply_reduce_fusion
  111.6 1.5 collective-permute-start.2
  113.1 5.1 %collective-permute-done.2 = f32[10,6,512]{2,0,1:T(8,128)S(1)} collective-permute-done((f32[10,6,512]{2,0,1:T(8,128)S(1)}, f32[10,6,512]{2,0,1:T(8,128)S(1)}, u32[]{:S(2)}, u32[]{:S(2)}) %collective-permute-start.2) | collective-permute-done | bytes 122912 | tf_op jit(solution)/shard_map/ppermute | solution.py:15
  118.2 0.3 fusion.12
  118.5 0.4 fusion.51
  118.9 1.9 collective-permute-start.3
  120.8 0.9 copy.52
  121.7 91.9 %psum.7 = f32[16,512]{1,0:T(8,128)S(1)} all-reduce(f32[16,512]{1,0:T(8,128)S(1)} %get-tuple-element.113), channel_id=1, replica_groups=mesh['river'=16,'hours'=32] {'river'}, use_global_device_ids=true, to_apply=%region_7.8 | all-reduce | flops 8192 | bytes 65536 | tf_op jit(solution)/shard_map/psum | solution.py:102
  213.7 0.6 add_minimum_fusion
  214.3 0.5 fusion.1
  214.8 2.7 fusion.63
  217.6 78.7 %all-gather.1 = f32[320,1,512]{2,1,0:T(1,128)S(1)} all-gather(f32[10,1,512]{2,1,0:T(1,128)S(1)} %copy.49), channel_id=3, replica_groups=mesh['river'=16,'hours'=32] {'hours'}, dimensions={0}, use_global_device_ids=true | all-gather | bytes 675840 | tf_op jit(solution)/shard_map/all_gather | solution.py:22
  296.3 1.6 reduce.1
  297.9 0.1 reshape.30
  298.0 0.8 copy-done
  298.8 0.4 minimum_subtract_fusion
  299.2 0.9 copy.54
  300.1 0.9 copy.53
  (68 shorter events, 0.6 us)
Async XLA Ops:
  91.9 8.6 %collective-permute-start = (f32[10,16,512]{2,0,1:T(8,128)S(1)}, f32[10,16,512]{2,0,1:T(8,128)S(1)}, u32[]{:S(2)}, u32[]{:S(2)}) collective-permute-start(f32[10,16,512]{2,0,1:T(8,128)S(1)} %reverse_add_fusion), channel_id=1, source_target_pairs={{32,0},{64,32},{96,64},{128,96},{160,128},{192,160},{224,192},{256... | collective-permute-start | bytes 983048 | tf_op jit(solution)/shard_map/ppermute | solution.py:15
  93.8 0.7 copy-start.7
  94.5 0.7 copy-start.8
  100.5 9.7 %copy-start.3 = (f32[10,16,512]{2,1,0:T(8,128)S(1)}, f32[10,16,512]{2,1,0:T(8,128)}, u32[]{:S(2)}) copy-start(f32[10,16,512]{2,1,0:T(8,128)} %param.20) | copy-start | bytes 983044
  101.0 1.5 copy-start.12
  101.0 9.2 %copy-start.2 = (f32[10,16,512]{2,1,0:T(8,128)S(1)}, f32[10,16,512]{2,1,0:T(8,128)}, u32[]{:S(2)}) copy-start(f32[10,16,512]{2,1,0:T(8,128)} %param.17) | copy-start | bytes 983044
  101.0 9.2 %copy-start.4 = (f32[16,512]{1,0:T(8,128)S(1)}, f32[16,512]{1,0:T(8,128)}, u32[]{:S(2)}) copy-start(f32[16,512]{1,0:T(8,128)} %param.19) | copy-start | bytes 98308
  101.1 9.1 %collective-permute-start.1 = (f32[10,6,512]{2,0,1:T(8,128)S(1)}, f32[10,6,512]{2,0,1:T(8,128)S(1)}, u32[]{:S(2)}, u32[]{:S(2)}) collective-permute-start(f32[10,6,512]{2,0,1:T(8,128)S(1)} %slice.66), channel_id=1, source_target_pairs={{1,0},{2,1},{3,2},{4,3},{5,4},{6,5},{7,6},{8,7},{9,8},{10,9},{11,1... | collective-permute-start | bytes 368648 | tf_op jit(solution)/shard_map/ppermute | solution.py:15
  110.2 0.7 copy-start.6
  111.6 6.5 %collective-permute-start.2 = (f32[10,6,512]{2,0,1:T(8,128)S(1)}, f32[10,6,512]{2,0,1:T(8,128)S(1)}, u32[]{:S(2)}, u32[]{:S(2)}) collective-permute-start(f32[10,6,512]{2,0,1:T(8,128)S(1)} %slice.77), channel_id=1, source_target_pairs={{0,1},{1,2},{2,3},{3,4},{4,5},{5,6},{6,7},{7,8},{8,9},{9,10},{10,1... | collective-permute-start | bytes 368648 | tf_op jit(solution)/shard_map/ppermute | solution.py:15
  118.9 95.4 %collective-permute-start.3 = (f32[10,16,512]{2,0,1:T(8,128)S(1)}, f32[10,16,512]{2,0,1:T(8,128)S(1)}, u32[]{:S(2)}, u32[]{:S(2)}) collective-permute-start(f32[10,16,512]{2,0,1:T(8,128)S(1)} %fusion.51), channel_id=1, source_target_pairs={{0,32},{32,64},{64,96},{96,128},{128,160},{160,192},{192,224},{224... | collective-permute-start | bytes 983048 | tf_op jit(solution)/shard_map/ppermute | solution.py:15
  120.8 93.5 %copy-start.1 = (f32[10,16,512]{2,1,0:T(8,128)S(1)}, f32[10,16,512]{2,1,0:T(8,128)}, u32[]{:S(2)}) copy-start(f32[10,16,512]{2,1,0:T(8,128)} %param.21) | copy-start | bytes 983044
  121.7 91.9 %copy-start.5 = (f32[16,512]{1,0:T(8,128)S(1)}, f32[16,512]{1,0:T(8,128)}, u32[]{:S(2)}) copy-start(f32[16,512]{1,0:T(8,128)} %param.22) | copy-start | bytes 98308
  297.9 1.0 copy-start
  298.0 0.8 copy-start.9
  298.0 0.8 copy-start.10
  298.0 0.8 copy-start.11
where the time goes:
time: 301 us
  blocking collectives  257 us (85%)
  waiting for transfers between devices  17.7 us (6%)
  other arithmetic  8.6 us (3%)
  local copies, waits for them, and re-layouts  7.67 us (3%)
  starting transfers between devices  6.72 us (2%)
    all_gather x2, blocking collectives, prefix(): gathered = lax.all_gather(part, axis)  165 us
    psum x1, blocking collectives, iterate(): supplied = lax.psum(partial_power, 'river')  91.9 us
    ppermute x4, waiting for transfers between devices, passed_along(): return lax.ppermute(block, axis, route)  17.7 us
    ppermute x4, starting transfers between devices, passed_along(): return lax.ppermute(block, axis, route)  6.72 us
  transfers between devices with their start and end apart: 4, of which 3 were waited for; matrix products, arithmetic and copies ran while one was open for 1% of the time, Pallas kernels for 0%

commit v1 on v0

--- a/solution.py
+++ b/solution.py
@@ -99,7 +99,7 @@
     )
     storage_excess = storage - jnp.clip(storage, lower_bound, upper_bound)
     partial_power = jnp.sum(scale_sum * efficiency[:, None, None] * extrapolated, 0)
-    supplied = lax.psum(partial_power, "river")
+    supplied = jnp.sum(lax.all_gather(partial_power, "river"), axis=0)
     demand_dual_new = jnp.minimum(demand_dual + dual_step * (supplied - demand), 0.0)
     return (release_new, storage_dual_new, demand_dual_new, storage_excess)
 

time: 301 us -> 240 us (0.80)
  blocking collectives: 257 us -> 195 us
    psum x1 -> x0, blocking collectives: 91.9 us -> none  [iterate(): supplied = lax.psum(partial_power, 'river')]
    all_gather x0 -> x1, blocking collectives: none -> 30.2 us  [iterate(): supplied = jnp.sum(lax.all_gather(partial_power, 'river'), axis=0)]
where the time goes in v1:
time: 240 us
  blocking collectives  195 us (81%)
  waiting for transfers between devices  17.7 us (7%)
  other arithmetic  8.63 us (4%)
  local copies, waits for them, and re-layouts  8.39 us (3%)
  starting transfers between devices  6.72 us (3%)
    all_gather x2, blocking collectives, prefix(): gathered = lax.all_gather(part, axis)  165 us
    all_gather x1, blocking collectives, iterate(): supplied = jnp.sum(lax.all_gather(partial_power, 'river'), axis=0)  30.2 us
    ppermute x4, waiting for transfers between devices, passed_along(): return lax.ppermute(block, axis, route)  17.7 us
    ppermute x4, starting transfers between devices, passed_along(): return lax.ppermute(block, axis, route)  6.72 us
    unnamed x29, local copies, waits for them, and re-layouts  6.26 us
  transfers between devices with their start and end apart: 4, of which 3 were waited for; matrix products, arithmetic and copies ran while one was open for 1% of the time, Pallas kernels for 0%

profile of v1, /device:TPU:32, one launch (start us, length us, event | category | flops | bytes accessed | tf_op | source)
XLA Modules:
  0.0 239.9 jit_solution(8353780990069071880)
XLA Ops:
  0.6 1.8 rev.7
  2.5 0.4 fusion.45
  2.9 86.1 %all-gather = f32[320,1,512]{2,1,0:T(1,128)S(1)} all-gather(f32[10,1,512]{2,1,0:T(1,128)S(1)} %copy.56), channel_id=2, replica_groups=mesh['river'=16,'hours'=32] {'hours'}, dimensions={0}, use_global_device_ids=true | all-gather | bytes 675840 | tf_op jit(solution)/shard_map/all_gather | solution.py:22
  89.0 1.6 reduce
  90.7 1.2 while.22
  91.9 1.9 collective-permute-start
  93.8 0.6 copy-done.7
  94.5 0.6 copy-done.8
  95.2 0.4 fusion.49
  95.6 4.9 %collective-permute-done = f32[10,16,512]{2,0,1:T(8,128)S(1)} collective-permute-done((f32[10,16,512]{2,0,1:T(8,128)S(1)}, f32[10,16,512]{2,0,1:T(8,128)S(1)}, u32[]{:S(2)}, u32[]{:S(2)}) %collective-permute-start) | collective-permute-done | bytes 327712 | tf_op jit(solution)/shard_map/ppermute | solution.py:15
  100.5 0.5 convolution_add_fusion.1
  101.1 1.4 collective-permute-start.1
  102.5 7.7 %collective-permute-done.1 = f32[10,6,512]{2,0,1:T(8,128)S(1)} collective-permute-done((f32[10,6,512]{2,0,1:T(8,128)S(1)}, f32[10,6,512]{2,0,1:T(8,128)S(1)}, u32[]{:S(2)}, u32[]{:S(2)}) %collective-permute-start.1) | collective-permute-done | bytes 122912 | tf_op jit(solution)/shard_map/ppermute | solution.py:15
  110.2 0.6 copy-done.6
  110.9 0.8 multiply_reduce_fusion
  111.6 1.5 collective-permute-start.2
  113.1 5.1 %collective-permute-done.2 = f32[10,6,512]{2,0,1:T(8,128)S(1)} collective-permute-done((f32[10,6,512]{2,0,1:T(8,128)S(1)}, f32[10,6,512]{2,0,1:T(8,128)S(1)}, u32[]{:S(2)}, u32[]{:S(2)}) %collective-permute-start.2) | collective-permute-done | bytes 122912 | tf_op jit(solution)/shard_map/ppermute | solution.py:15
  118.2 0.3 fusion.12
  118.5 0.4 fusion.51
  118.9 1.9 collective-permute-start.3
  120.8 30.2 %all-gather.2 = f32[256,512]{1,0:T(8,128)S(1)} all-gather(f32[16,512]{1,0:T(8,128)S(1)} %get-tuple-element.117), channel_id=4, replica_groups=mesh['river'=16,'hours'=32] {'river'}, dimensions={0}, use_global_device_ids=true | all-gather | bytes 557056 | tf_op jit(solution)/shard_map/all_gather | solution.py:102
  151.0 0.9 copy.66
  151.9 0.7 copy-done.5
  152.7 0.6 add_minimum_fusion
  153.3 0.5 fusion.1
  153.8 2.7 %fusion.63 = f32[10,16,512]{2,0,1:T(8,128)S(1)} fusion(f32[10,16,512]{2,0,1:T(8,128)S(1)} %fusion.1), kind=kOutput, calls=%fused_computation.105 | output fusion | flops 1228800 | bytes 655360 | tf_op jit(solution)/shard_map/jit(cumsum)/reduce_window_sum | solution.py:147
  156.6 78.6 %all-gather.1 = f32[320,1,512]{2,1,0:T(1,128)S(1)} all-gather(f32[10,1,512]{2,1,0:T(1,128)S(1)} %copy.63), channel_id=3, replica_groups=mesh['river'=16,'hours'=32] {'hours'}, dimensions={0}, use_global_device_ids=true | all-gather | bytes 675840 | tf_op jit(solution)/shard_map/all_gather | solution.py:22
  235.2 1.6 reduce.1
  236.9 0.8 copy-done
  237.7 0.4 minimum_subtract_fusion
  238.1 0.9 copy.68
  239.0 0.9 copy.67
  (69 shorter events, 0.8 us)
Async XLA Ops:
  91.9 8.6 %collective-permute-start = (f32[10,16,512]{2,0,1:T(8,128)S(1)}, f32[10,16,512]{2,0,1:T(8,128)S(1)}, u32[]{:S(2)}, u32[]{:S(2)}) collective-permute-start(f32[10,16,512]{2,0,1:T(8,128)S(1)} %reverse_add_fusion), channel_id=1, source_target_pairs={{32,0},{64,32},{96,64},{128,96},{160,128},{192,160},{224,192},{256... | collective-permute-start | bytes 983048 | tf_op jit(solution)/shard_map/ppermute | solution.py:15
  93.8 0.7 copy-start.7
  94.5 0.7 copy-start.8
  100.5 9.7 %copy-start.3 = (f32[10,16,512]{2,1,0:T(8,128)S(1)}, f32[10,16,512]{2,1,0:T(8,128)}, u32[]{:S(2)}) copy-start(f32[10,16,512]{2,1,0:T(8,128)} %param.20) | copy-start | bytes 983044
  101.0 1.5 copy-start.12
  101.0 9.2 %copy-start.2 = (f32[10,16,512]{2,1,0:T(8,128)S(1)}, f32[10,16,512]{2,1,0:T(8,128)}, u32[]{:S(2)}) copy-start(f32[10,16,512]{2,1,0:T(8,128)} %param.17) | copy-start | bytes 983044
  101.0 9.2 %copy-start.4 = (f32[16,512]{1,0:T(8,128)S(1)}, f32[16,512]{1,0:T(8,128)}, u32[]{:S(2)}) copy-start(f32[16,512]{1,0:T(8,128)} %param.19) | copy-start | bytes 98308
  101.1 9.1 %collective-permute-start.1 = (f32[10,6,512]{2,0,1:T(8,128)S(1)}, f32[10,6,512]{2,0,1:T(8,128)S(1)}, u32[]{:S(2)}, u32[]{:S(2)}) collective-permute-start(f32[10,6,512]{2,0,1:T(8,128)S(1)} %slice.66), channel_id=1, source_target_pairs={{1,0},{2,1},{3,2},{4,3},{5,4},{6,5},{7,6},{8,7},{9,8},{10,9},{11,1... | collective-permute-start | bytes 368648 | tf_op jit(solution)/shard_map/ppermute | solution.py:15
  110.2 0.7 copy-start.6
  111.6 6.5 %collective-permute-start.2 = (f32[10,6,512]{2,0,1:T(8,128)S(1)}, f32[10,6,512]{2,0,1:T(8,128)S(1)}, u32[]{:S(2)}, u32[]{:S(2)}) collective-permute-start(f32[10,6,512]{2,0,1:T(8,128)S(1)} %slice.77), channel_id=1, source_target_pairs={{0,1},{1,2},{2,3},{3,4},{4,5},{5,6},{6,7},{7,8},{8,9},{9,10},{10,1... | collective-permute-start | bytes 368648 | tf_op jit(solution)/shard_map/ppermute | solution.py:15
  118.9 34.4 %collective-permute-start.3 = (f32[10,16,512]{2,0,1:T(8,128)S(1)}, f32[10,16,512]{2,0,1:T(8,128)S(1)}, u32[]{:S(2)}, u32[]{:S(2)}) collective-permute-start(f32[10,16,512]{2,0,1:T(8,128)S(1)} %fusion.51), channel_id=1, source_target_pairs={{0,32},{32,64},{64,96},{96,128},{128,160},{160,192},{192,224},{224... | collective-permute-start | bytes 983048 | tf_op jit(solution)/shard_map/ppermute | solution.py:15
  151.9 0.8 copy-start.5
  151.9 1.4 copy-start.1
  236.7 1.0 copy-start
  236.9 0.8 copy-start.9
  236.9 0.8 copy-start.10
  236.9 0.8 copy-start.11
